TPU v7x, 32 devices: a whole 2x2x4 slice. The times are simulated.
32 devices in a mesh: groups: 2 (over y), frame: 4 (over z), head: 2 (over x), seq: 2 (over core).
Axes of the slice: x: 2, y: 2, z: 4, core: 2. Of those that a mesh axis runs over, the one named last changes fastest.
Arguments:
- queries: bfloat16 [32, 1024, 1280], P(('groups', 'frame'), 'seq', 'head'), parts along dimension 0, may hold values from -240 to 240
- key_states: bfloat16 [32, 1024, 1280], P(('groups', 'frame'), 'seq', 'head'), parts along dimension 0, may hold values from -6.5 to 6.5
- value_states: bfloat16 [32, 1024, 1280], P(('groups', 'frame'), 'seq', 'head'), parts along dimension 0, may hold values from -6 to 6
Outputs:
- attended: bfloat16 [32, 1024, 1280], P(('groups', 'frame'), 'seq', 'head'), parts along dimension 0
There are 2 independent parts, one for each index of `groups`. A program takes and returns all parts, laid end to end along the dimension named above; each array names one. Nothing has to cross between parts.
All inputs are finite; a program needn't handle non-finite values.
Results may differ from a plain program's by a relative error of at most 0.0075.
Values may be sent and summed in bfloat16 or wider, within the bound.
A program may use at most 128 MiB of HBM per device.

v0:
```python
import jax
import jax.numpy as jnp
from jax import lax
from jax.experimental import pallas as pl
from jax.experimental.pallas import tpu as pltpu
from jax.sharding import PartitionSpec as P

HEAD_DIM = 64
LANES = 128


def from_behind(value, axis, steps):
    count = lax.axis_size(axis)
    first, last = (max(0, -steps), min(count, count - steps))
    return lax.ppermute(value, axis, [(source, source + steps) for source in range(first, last)])


def spread(x, axis, root):
    mine = lax.axis_index(axis) == root
    return lax.psum(jnp.where(mine, x, jnp.zeros_like(x)), axis)


def attend_columns(q, keys, values):
    width = q.shape[1]
    head_of_lane = lax.broadcasted_iota(jnp.int32, q.shape, 1) // HEAD_DIM
    scaled = q * jnp.asarray(HEAD_DIM**-0.5, q.dtype)
    summed = [jnp.concatenate([v, jnp.ones_like(v)], 1) for v in values]
    result = None
    for head in range(width // HEAD_DIM):
        one = jnp.where(head_of_lane == head, scaled, jnp.zeros_like(scaled))
        scores = [
            lax.dot_general(one, k, (((1,), (1,)), ((), ())), preferred_element_type=jnp.float32)
            for k in keys
        ]
        row_max = jnp.max(scores[0], axis=1, keepdims=True)
        for s in scores[1:]:
            row_max = jnp.maximum(row_max, jnp.max(s, axis=1, keepdims=True))
        total = None
        for s, v in zip(scores, summed):
            rounded = jnp.exp(s - row_max).astype(jnp.bfloat16)
            part = jnp.dot(rounded, v, preferred_element_type=jnp.float32)
            total = part if total is None else total + part
        out = total[:, :width] / total[:, width:]
        result = out if result is None else jnp.where(head_of_lane == head, out, result)
    return result.astype(jnp.bfloat16)


def frame_kernel(q_ref, ka_ref, va_ref, kp_ref, vp_ref, o_ref):
    rows, columns = q_ref.shape[1:]
    block = min(rows, 256)

    def one(first, width, row):
        at = pl.ds(first, width)
        rows_at = pl.ds(pl.multiple_of(row * block, block), block)
        o_ref[0, rows_at, at] = attend_columns(
            q_ref[0, rows_at, at],
            [ka_ref[:, at], kp_ref[0, :, at]],
            [va_ref[:, at], vp_ref[0, :, at]],
        )

    pairs = columns // LANES
    blocks = rows // block

    @pl.loop(0, pairs * blocks)
    def _(step):
        one(pl.multiple_of((step // blocks) * LANES, LANES), LANES, step % blocks)

    if columns % LANES:

        @pl.loop(0, blocks)
        def _(step):
            one(pairs * LANES, columns % LANES, step)


def local(queries, key_states, value_states):
    frames, rows, columns = queries.shape
    at_root = lax.axis_index("frame") == 0
    key_value = jnp.stack([key_states, value_states], 0)
    whole = lax.all_gather(key_value, "seq", axis=2, tiled=True)
    shifted = from_behind(whole[:, frames - 1], "frame", 1)
    anchor = spread(whole[:, 0], "frame", 0)
    prior = jnp.where(at_root, anchor, shifted)
    previous = jnp.concatenate([prior[:, None], whole[:, : frames - 1]], 1)
    tokens = whole.shape[2]
    mine = pl.BlockSpec((1, rows, columns), lambda f: (f, 0, 0))
    first = pl.BlockSpec((tokens, columns), lambda f: (0, 0))
    before = pl.BlockSpec((1, tokens, columns), lambda f: (f, 0, 0))
    return pl.pallas_call(
        frame_kernel,
        grid=(frames,),
        out_shape=jax.ShapeDtypeStruct(queries.shape, queries.dtype),
        in_specs=[mine, first, first, before, before],
        out_specs=mine,
        compiler_params=pltpu.CompilerParams(vmem_limit_bytes=48 * 1024 * 1024),
    )(queries, anchor[0], anchor[1], previous[0], previous[1])


def solution(mesh):
    spec = P(("groups", "frame"), "seq", "head")
    return jax.shard_map(
        local, mesh=mesh, in_specs=(spec, spec, spec), out_specs=spec, check_vma=False
    )
```

profile of v0, /device:TPU:24, one launch (start us, length us, event | category | flops | bytes accessed | tf_op | source)
XLA Modules:
  0.0 286.1 jit_solution(2113103862604142521)
XLA Ops:
  6.5 0.0 all-gather.2.cloned.1.call-start
  6.5 5.4 %pad_maximum_fusion.1 = bf16[2,4,512,640]{3,2,1,0:T(8,128)(2,1)} fusion(bf16[1,4,512,640]{3,2,1,0:T(8,128)(2,1)} %bitcast.24, bf16[1,4,512,640]{3,2,1,0:T(8,128)(2,1)} %bitcast.25), kind=kLoop, calls=%fused_computation.6 | loop fusion | flops 2621440 | bytes 10485760 | tf_op jit(solution)/shard_map/stack | solution.py:78
  12.0 0.0 all-gather.2.cloned.1.call-update
  12.0 0.0 all-reduce.2.cloned.1.call-start
  12.1 23.9 %all-gather.2.cloned.1.call-done = bf16[2,4,1024,640]{3,2,1,0:T(8,128)(2,1)} async-done(((bf16[2,4,512,640]{3,2,1,0:T(8,128)(2,1)}), bf16[2,4,1024,640]{3,2,1,0:T(8,128)(2,1)}) %all-gather.2.cloned.1.call-update) | async-done | bytes 10485776 | tf_op jit(solution)/shard_map/all_gather | solution.py:79
  36.0 3.5 %fusion.4 = bf16[2,1024,640]{2,1,0:T(8,128)(2,1)} fusion(bf16[2,4,1024,640]{3,2,1,0:T(8,128)(2,1)} %all-gather.2.cloned.1.call-done, pred[]{:T(512)S(6)} %eq.4), kind=kLoop, calls=%fused_computation.10 | loop fusion | flops 1310720 | bytes 5242881 | tf_op jit(solution)/shard_map/jit(_where)/select_n | solution.py:20
  39.4 0.0 all-reduce.2.cloned.1.call-update
  39.4 3.4 %slice_bitcast_fusion = bf16[2,1024,640]{2,1,0:T(8,128)(2,1)} fusion(bf16[2,4,1024,640]{3,2,1,0:T(8,128)(2,1)} %all-gather.2.cloned.1.call-done), kind=kLoop, calls=%fused_computation.7 | loop fusion | bytes 5242880 | tf_op jit(solution)/shard_map/squeeze | solution.py:80
  42.9 1.3 collective-permute-start
  44.1 143.6 %all-reduce.2.cloned.1.call-done = bf16[2,1024,640]{2,1,0:T(8,128)(2,1)} async-done(((bf16[2,1024,640]{2,1,0:T(8,128)(2,1)}), bf16[2,1024,640]{2,1,0:T(8,128)(2,1)}) %all-reduce.2.cloned.1.call-update) | async-done | bytes 2621456 | tf_op jit(solution)/shard_map/psum | solution.py:20
  187.8 0.0 slice-start
  187.8 0.0 collective-permute-done
  187.8 0.3 select_bitcast_fusion
  188.1 2.9 %slice-done = bf16[2,3,1024,640]{3,2,1,0:T(8,128)(2,1)S(1)} async-done(((bf16[2,4,1024,640]{3,2,1,0:T(8,128)(2,1)}), bf16[2,3,1024,640]{3,2,1,0:T(8,128)(2,1)S(1)}, s32[]{:S(2)}) %slice-start) | async-done | bytes 7864344 | tf_op jit(solution)/shard_map/slice | solution.py:83
  191.0 0.0 copy-start.1
  191.0 4.4 %fusion.2 = (bf16[4,1024,640]{2,1,0:T(8,128)(2,1)}, bf16[4,1024,640]{2,1,0:T(8,128)(2,1)}) fusion(bf16[2,3,1024,640]{3,2,1,0:T(8,128)(2,1)S(1)} %slice-done, bf16[2,1,1024,640]{3,2,1,0:T(8,128)(2,1)S(1)} %select_bitcast_fusion), kind=kLoop, calls=%fused_computation.5 | loop fusion | flops 5242880 | bytes 20971520 | tf_op jit(solution)/shard_map/squeeze | solution.py:95
  195.4 0.0 copy-done.1
  195.4 0.0 copy-start
  195.4 0.2 slice_bitcast_fusion.2
  195.6 1.5 copy-done
  197.1 82.1 %shard_map.37 = bf16[4,512,640]{2,1,0:T(8,128)(2,1)} custom-call(bf16[4,512,640]{2,1,0:T(8,128)(2,1)S(1)} %copy-done, bf16[1024,640]{1,0:T(8,128)(2,1)S(1)} %get-tuple-element.8.ka_ref, bf16[1024,640]{1,0:T(8,128)(2,1)S(1)} %get-tuple-element.7.va_ref, bf16[4,1024,640]{2,1,0:T(8,128)(2,1)} %get-tuple-element.6.kp_ref, ...), custom_call_target="tpu_custom_call" | custom-call | tf_op jit(solution)/shard_map/pallas_call | solution.py:88
Async XLA Ops:
  6.5 29.4 %all-gather.2.cloned.1.call-start = ((), (), s32[]{:S(2)}) async-start(), calls=%async_computation | async-start | bytes 15728640 | tf_op jit(solution)/shard_map/all_gather | solution.py:79
  12.0 175.8 %all-reduce.2.cloned.1.call-start = ((), (), s32[]{:S(2)}) async-start(), calls=%async_computation.1 | async-start | bytes 5242880 | tf_op jit(solution)/shard_map/psum | solution.py:20
  42.9 144.9 %collective-permute-start = (bf16[2,1024,640]{2,1,0:T(8,128)(2,1)}, bf16[2,1024,640]{2,1,0:T(8,128)(2,1)S(1)}, u32[]{:S(2)}, u32[]{:S(2)}) collective-permute-start(bf16[2,1024,640]{2,1,0:T(8,128)(2,1)} %slice_bitcast_fusion), channel_id=1, source_target_pairs={{0,4},{4,8},{8,12},{1,5},{5,9},{9,13},{2,6},{6,10},{10,14},{3,7},{... | collective-permute-start | bytes 7864328 | tf_op jit(solution)/shard_map/ppermute | solution.py:15
  187.8 3.2 %slice-start = ((bf16[2,4,1024,640]{3,2,1,0:T(8,128)(2,1)}), bf16[2,3,1024,640]{3,2,1,0:T(8,128)(2,1)S(1)}, s32[]{:S(2)}) async-start(bf16[2,4,1024,640]{3,2,1,0:T(8,128)(2,1)} %all-gather.2.cloned.1.call-done), calls=%async_computation.2 | async-start | bytes 15728640 | tf_op jit(solution)/shard_map/slice | solution.py:83
  191.0 4.4 %copy-start.1 = (bf16[2,1024,640]{2,1,0:T(8,128)(2,1)S(1)}, bf16[2,1024,640]{2,1,0:T(8,128)(2,1)}, u32[]{:S(2)}) copy-start(bf16[2,1024,640]{2,1,0:T(8,128)(2,1)} %all-reduce.2.cloned.1.call-done) | copy-start | bytes 7864324
  195.4 1.7 copy-start
Sparse Core Ops, SparseCore 0:
  12.1 23.7 all-gather.1
  39.6 148.1 all-reduce.1
where the time goes:
time: 288 us; the launch traced here: 286 us
  waiting for transfers between devices  168 us (58%)
  Pallas kernels  82.1 us (29%)
  other arithmetic  13.6 us (5%)
  between operations  13.4 us (5%)
  local copies, waits for them, and re-layouts  8.11 us (3%)
    psum x1, waiting for transfers between devices, spread(): return lax.psum(jnp.where(mine, x, jnp.zeros_like(x)), axis)  144 us
    pallas_call x1, Pallas kernels, local(): pl.pallas_call(frame_kernel, grid=(frames,), out_shape=jax.ShapeDtypeStru...  82.1 us
    all_gather x1, waiting for transfers between devices, local(): whole = lax.all_gather(key_value, 'seq', axis=2, tiled=True)  23.9 us
  transfers between devices with their start and end apart: 3, of which 2 were waited for; matrix products, arithmetic and copies ran while one was open for 1% of the time, Pallas kernels for 0%

commit v1 on v0

v1 whole, which is shorter than its diff:
```python
import functools

import jax
import jax.numpy as jnp
from jax import lax
from jax.experimental import pallas as pl
from jax.experimental.pallas import tpu as pltpu
from jax.sharding import PartitionSpec as P

HEAD_DIM = 64
LANES = 128


def attend_columns(q, keys, values):
    width = q.shape[1]
    head_of_lane = lax.broadcasted_iota(jnp.int32, q.shape, 1) // HEAD_DIM
    scaled = q * jnp.asarray(HEAD_DIM**-0.5, q.dtype)
    summed = [jnp.concatenate([v, jnp.ones_like(v)], 1) for v in values]
    result = None
    for head in range(width // HEAD_DIM):
        one = jnp.where(head_of_lane == head, scaled, jnp.zeros_like(scaled))
        scores = [
            lax.dot_general(one, k, (((1,), (1,)), ((), ())), preferred_element_type=jnp.float32)
            for k in keys
        ]
        row_max = jnp.max(scores[0], axis=1, keepdims=True)
        for s in scores[1:]:
            row_max = jnp.maximum(row_max, jnp.max(s, axis=1, keepdims=True))
        total = None
        for s, v in zip(scores, summed):
            rounded = jnp.exp(s - row_max).astype(jnp.bfloat16)
            part = jnp.dot(rounded, v, preferred_element_type=jnp.float32)
            total = part if total is None else total + part
        out = total[:, :width] / total[:, width:]
        result = out if result is None else jnp.where(head_of_lane == head, out, result)
    return result.astype(jnp.bfloat16)


def kernel(
    blocks,
    halves,
    q_ref,
    k_ref,
    v_ref,
    o_ref,
    k_buf,
    v_buf,
    own_sem,
    swap_send,
    swap_recv,
    prior_send,
    prior_recv,
    anchor_send,
    anchor_recv,
    relay_send,
    relay_recv,
):
    frames, rows, columns = q_ref.shape
    chunks = own_sem.shape[1]
    width = columns // chunks
    anchor_slot, prior_slot = frames, frames + 1
    z = lax.axis_index("frame")
    half = lax.axis_index("seq")
    later = (z + blocks - 1) // blocks
    ahead = {"frame": (z + 1) % blocks}
    first = z == 0
    sends_on = z < blocks - 1
    mine = pl.ds(pl.multiple_of(half * rows, rows), rows)
    sources, buffers = (k_ref, v_ref), (k_buf, v_buf)
    offsets = range(1, halves)

    def cols(c):
        return pl.ds(pl.multiple_of(c * width, LANES), width) if chunks > 1 else pl.ds(0, width)

    def sibling(j):
        return {"seq": (half + j) % halves}

    def remote(src, dst, send, recv, where):
        return pltpu.make_async_remote_copy(
            src_ref=src,
            dst_ref=dst,
            send_sem=send,
            recv_sem=recv,
            device_id=where,
            device_id_type=pl.DeviceIdType.MESH,
        )

    def own(i, c):
        return pltpu.make_async_copy(
            sources[i].at[pl.ds(0, frames - 1), :, cols(c)],
            buffers[i].at[pl.ds(0, frames - 1), mine, cols(c)],
            own_sem.at[i, c],
        )

    def swap(i, c, j):
        return remote(
            sources[i].at[pl.ds(0, frames - 1), :, cols(c)],
            buffers[i].at[pl.ds(0, frames - 1), mine, cols(c)],
            swap_send.at[i, c, j - 1],
            swap_recv.at[i, c, j - 1],
            sibling(j),
        )

    def prior(i, c):
        return remote(
            sources[i].at[frames - 1, :, cols(c)],
            buffers[i].at[prior_slot, mine, cols(c)],
            prior_send.at[i, c],
            prior_recv.at[i, c],
            ahead,
        )

    def anchor(i, c, root):
        here = buffers[i].at[anchor_slot, mine, cols(c)]
        return remote(
            sources[i].at[0, :, cols(c)] if root else here,
            here,
            anchor_send.at[i, c],
            anchor_recv.at[i, c],
            ahead,
        )

    def relay(which, i, c, j):
        here = buffers[i].at[anchor_slot + which, mine, cols(c)]
        return remote(
            here,
            here,
            relay_send.at[which, i, c, j - 1],
            relay_recv.at[which, i, c, j - 1],
            sibling(j),
        )

    barrier = pltpu.get_barrier_semaphore()

    @pl.when(sends_on)
    def _():
        pl.semaphore_signal(
            barrier, inc=1, device_id=ahead, device_id_type=pl.DeviceIdType.MESH
        )

    @pl.when(z > 0)
    def _():
        pl.semaphore_signal(
            barrier,
            inc=1,
            device_id={"frame": (z + blocks - 1) % blocks},
            device_id_type=pl.DeviceIdType.MESH,
        )

    for j in offsets:
        pl.semaphore_signal(
            barrier, inc=1, device_id=sibling(j), device_id_type=pl.DeviceIdType.MESH
        )
    pl.semaphore_wait(barrier, later + 1 - (z + 1) // blocks + halves - 1)

    @pl.when(first & sends_on)
    def _():
        @pl.loop(0, chunks)
        def _(c):
            for i in range(2):
                anchor(i, c, True).start()
            for i in range(2):
                prior(i, c).start()

    @pl.when((z > 0) & sends_on)
    def _():
        for i in range(2):
            prior(i, 0).start()

    @pl.loop(0, chunks)
    def _(c):
        for i in range(2):
            own(i, c).start()
            for j in offsets:
                swap(i, c, j).start()

    def receive(c):
        @pl.when(z > 0)
        def _():
            for i in range(2):
                anchor(i, c, False).wait_recv()

                @pl.when(sends_on)
                def _():
                    anchor(i, c, False).start()

                for j in offsets:
                    relay(0, i, c, j).start()

            @pl.when(sends_on & (c + 1 < chunks))
            def _():
                for i in range(2):
                    prior(i, c + 1).start()

            for i in range(2):
                prior(i, c).wait_recv()
                for j in offsets:
                    relay(1, i, c, j).start()

    def complete(c):
        for i in range(2):
            own(i, c).wait()
            for j in offsets:
                swap(i, c, j).wait_recv()

        @pl.when(z > 0)
        def _():
            for i in range(2):
                for j in offsets:
                    relay(0, i, c, j).wait_recv()
                    relay(1, i, c, j).wait_recv()

    block = min(rows, 256)
    per_frame = rows // block
    steps = frames * per_frame

    def compute(c, step):
        frame = step // per_frame
        opens = (frames - frame) // frames
        before = (frame - 1) * (1 - opens) + opens * later * prior_slot
        zero = later * anchor_slot
        at_rows = pl.ds(pl.multiple_of((step % per_frame) * block, block), block)
        for start in range(0, width, LANES):
            size = min(LANES, width - start)
            if chunks > 1:
                at = cols(c)
            else:
                at = pl.ds(start, size)
            o_ref[frame, at_rows, at] = attend_columns(
                q_ref[frame, at_rows, at],
                [k_buf[zero, :, at], k_buf[before, :, at]],
                [v_buf[zero, :, at], v_buf[before, :, at]],
            )

    receive(0)

    @pl.loop(0, chunks)
    def _(c):
        complete(c)

        @pl.loop(0, steps)
        def _(step):
            @pl.when((step == steps // 2) & (c + 1 < chunks))
            def _():
                receive(c + 1)

            compute(c, step)

    @pl.loop(0, chunks)
    def _(c):
        for i in range(2):
            for j in offsets:
                swap(i, c, j).wait_send()

            @pl.when(sends_on)
            def _():
                prior(i, c).wait_send()
                anchor(i, c, False).wait_send()

            @pl.when(z > 0)
            def _():
                for j in offsets:
                    relay(0, i, c, j).wait_send()
                    relay(1, i, c, j).wait_send()


def local(blocks, halves, queries, key_states, value_states):
    frames, rows, columns = queries.shape
    chunks = columns // LANES if columns % LANES == 0 else 1
    held = pltpu.VMEM((frames + 2, rows * halves, columns), queries.dtype)
    dma = pltpu.SemaphoreType.DMA
    plain = dma((2, chunks))
    across = dma((2, chunks, halves - 1))
    relays = dma((2, 2, chunks, halves - 1))
    anywhere = pl.BlockSpec(memory_space=pl.ANY)
    near = pl.BlockSpec(memory_space=pltpu.VMEM)
    return pl.pallas_call(
        functools.partial(kernel, blocks, halves),
        out_shape=jax.ShapeDtypeStruct(queries.shape, queries.dtype),
        in_specs=[near, anywhere, anywhere],
        out_specs=near,
        scratch_shapes=[
            held,
            held,
            plain,
            across,
            across,
            plain,
            plain,
            plain,
            plain,
            relays,
            relays,
        ],
        compiler_params=pltpu.CompilerParams(
            collective_id=0, has_side_effects=True, vmem_limit_bytes=56 * 1024 * 1024
        ),
    )(queries, key_states, value_states)


def solution(mesh):
    spec = P(("groups", "frame"), "seq", "head")
    body = functools.partial(local, mesh.shape["frame"], mesh.shape["seq"])
    return jax.shard_map(
        body, mesh=mesh, in_specs=(spec, spec, spec), out_specs=spec, check_vma=False
    )
```

time: 288 us -> 120 us (0.42)
  waiting for transfers between devices: 168 us -> 0 us
  Pallas kernels: 82.1 us -> 117 us
  other arithmetic: 13.6 us -> 0 us
  between operations: 13.4 us -> 0.01 us
  local copies, waits for them, and re-layouts: 8.11 us -> 3.46 us
    psum x1 -> x0, waiting for transfers between devices: 144 us -> none  [spread(): return lax.psum(jnp.where(mine, x, jnp.zeros_like(x)), axis)]
    pallas_call x1, Pallas kernels: 82.1 us -> 117 us  [local(): pl.pallas_call(functools.partial(kernel, blocks, halves), out_shape=jax.S...]
    all_gather x1 -> x0, waiting for transfers between devices: 23.9 us -> none  [local(): whole = lax.all_gather(key_value, 'seq', axis=2, tiled=True)]
    another operation x1 -> x0, other arithmetic: 5.45 us -> none  [local(): key_value = jnp.stack([key_states, value_states], 0)]
    squeeze x1 -> x0, other arithmetic: 4.39 us -> none  [local(): previous[1]]
    squeeze x2 -> x0, local copies, waits for them, and re-layouts: 3.64 us -> none  [the longest x1 3.42 us: local(): shifted = from_behind(whole[:, frames - 1], 'frame', 1)]
    select_n x1 -> x0, other arithmetic: 3.46 us -> none  [spread(): return lax.psum(jnp.where(mine, x, jnp.zeros_like(x)), axis)]
    slice x2 -> x0, local copies, waits for them, and re-layouts: 2.95 us -> none  [local(): previous = jnp.concatenate([prior[:, None], whole[:, :frames - 1]], 1)]
  transfers between devices with their start and end apart: 3 -> 0, of which waited for: 2 -> 0; matrix products, arithmetic and copies ran while one was open for 1% -> 0% of each run, Pallas kernels for 0% -> 0%
where the time goes in v1:
time: 120 us
  Pallas kernels  117 us (98%)
  local copies, waits for them, and re-layouts  3.46 us (3%)
    pallas_call x1, Pallas kernels, local(): pl.pallas_call(functools.partial(kernel, blocks, halves), out_shape=jax.S...  117 us
    unnamed x1, local copies, waits for them, and re-layouts  3.46 us

profile of v1, /device:TPU:24, one launch (start us, length us, event | category | flops | bytes accessed | tf_op | source)
XLA Modules:
  0.0 120.2 jit_solution(10110147363155358714)
XLA Ops:
  0.0 116.8 %shard_map.37 = bf16[4,512,640]{2,1,0:T(8,128)(2,1)} custom-call(bf16[4,512,640]{2,1,0:T(8,128)(2,1)} %q_ref.1, bf16[4,512,640]{2,1,0:T(8,128)(2,1)} %k_ref.1, bf16[4,512,640]{2,1,0:T(8,128)(2,1)} %v_ref.1), custom_call_target="tpu_custom_call" | custom-call | tf_op jit(solution)/shard_map/pallas_call | solution.py:277
  116.8 3.5 %copy.5 = bf16[4,512,640]{2,1,0:T(8,128)(2,1)} copy(bf16[4,512,640]{2,1,0:T(8,128)(2,1)} %shard_map.37) | data formatting | bytes 5242880

commit v2 on v1

--- a/solution.py
+++ b/solution.py
@@ -9,30 +9,36 @@
 
 HEAD_DIM = 64
 LANES = 128
+KEY_BLOCK = 512
 
 
 def attend_columns(q, keys, values):
-    width = q.shape[1]
+    rows, width = q.shape
+    heads = width // HEAD_DIM
     head_of_lane = lax.broadcasted_iota(jnp.int32, q.shape, 1) // HEAD_DIM
     scaled = q * jnp.asarray(HEAD_DIM**-0.5, q.dtype)
-    summed = [jnp.concatenate([v, jnp.ones_like(v)], 1) for v in values]
-    result = None
-    for head in range(width // HEAD_DIM):
-        one = jnp.where(head_of_lane == head, scaled, jnp.zeros_like(scaled))
-        scores = [
-            lax.dot_general(one, k, (((1,), (1,)), ((), ())), preferred_element_type=jnp.float32)
-            for k in keys
-        ]
-        row_max = jnp.max(scores[0], axis=1, keepdims=True)
-        for s in scores[1:]:
-            row_max = jnp.maximum(row_max, jnp.max(s, axis=1, keepdims=True))
-        total = None
-        for s, v in zip(scores, summed):
-            rounded = jnp.exp(s - row_max).astype(jnp.bfloat16)
-            part = jnp.dot(rounded, v, preferred_element_type=jnp.float32)
-            total = part if total is None else total + part
-        out = total[:, :width] / total[:, width:]
-        result = out if result is None else jnp.where(head_of_lane == head, out, result)
+    stacked = jnp.concatenate(
+        [jnp.where(head_of_lane == h, scaled, jnp.zeros_like(scaled)) for h in range(heads)], 0
+    )
+    row_max = total = None
+    for k, v in zip(keys, values):
+        for start in range(0, k.shape[0], KEY_BLOCK):
+            k_part, v_part = k[start : start + KEY_BLOCK], v[start : start + KEY_BLOCK]
+            summed = jnp.concatenate([v_part, jnp.ones_like(v_part)], 1)
+            scores = lax.dot_general(
+                stacked, k_part, (((1,), (1,)), ((), ())), preferred_element_type=jnp.float32
+            )
+            newer = jnp.max(scores, axis=1, keepdims=True)
+            if row_max is not None:
+                newer = jnp.maximum(row_max, newer)
+            rounded = jnp.exp(scores - newer).astype(jnp.bfloat16)
+            part = jnp.dot(rounded, summed, preferred_element_type=jnp.float32)
+            total = part if row_max is None else total * jnp.exp(row_max - newer) + part
+            row_max = newer
+    out = total[:, :width] / total[:, width:]
+    result = out[:rows]
+    for h in range(1, heads):
+        result = jnp.where(head_of_lane == h, out[h * rows : (h + 1) * rows], result)
     return result.astype(jnp.bfloat16)
 
 
@@ -210,7 +216,7 @@
                     relay(0, i, c, j).wait_recv()
                     relay(1, i, c, j).wait_recv()
 
-    block = min(rows, 256)
+    block = min(rows, 512)
     per_frame = rows // block
     steps = frames * per_frame
 

time: 120 us -> 101 us (0.84)
  Pallas kernels: 117 us -> 97.1 us
    pallas_call x1, Pallas kernels: 117 us -> 97.1 us  [local(): pl.pallas_call(functools.partial(kernel, blocks, halves), out_shape=jax.S...]
where the time goes in v2:
time: 101 us
  Pallas kernels  97.1 us (96%)
  local copies, waits for them, and re-layouts  3.46 us (3%)
    pallas_call x1, Pallas kernels, local(): pl.pallas_call(functools.partial(kernel, blocks, halves), out_shape=jax.S...  97.1 us
    unnamed x1, local copies, waits for them, and re-layouts  3.46 us

profile of v2, /device:TPU:24, one launch (start us, length us, event | category | flops | bytes accessed | tf_op | source)
XLA Modules:
  0.0 100.5 jit_solution(8585394226765065639)
XLA Ops:
  0.0 97.1 %shard_map.37 = bf16[4,512,640]{2,1,0:T(8,128)(2,1)} custom-call(bf16[4,512,640]{2,1,0:T(8,128)(2,1)} %q_ref.1, bf16[4,512,640]{2,1,0:T(8,128)(2,1)} %k_ref.1, bf16[4,512,640]{2,1,0:T(8,128)(2,1)} %v_ref.1), custom_call_target="tpu_custom_call" | custom-call | tf_op jit(solution)/shard_map/pallas_call | solution.py:283
  97.1 3.5 %copy.5 = bf16[4,512,640]{2,1,0:T(8,128)(2,1)} copy(bf16[4,512,640]{2,1,0:T(8,128)(2,1)} %shard_map.37) | data formatting | bytes 5242880

commit v3 on v2

--- a/solution.py
+++ b/solution.py
@@ -12,15 +12,19 @@
 KEY_BLOCK = 512
 
 
-def attend_columns(q, keys, values):
-    rows, width = q.shape
-    heads = width // HEAD_DIM
+def stack_heads(q):
     head_of_lane = lax.broadcasted_iota(jnp.int32, q.shape, 1) // HEAD_DIM
     scaled = q * jnp.asarray(HEAD_DIM**-0.5, q.dtype)
-    stacked = jnp.concatenate(
-        [jnp.where(head_of_lane == h, scaled, jnp.zeros_like(scaled)) for h in range(heads)], 0
+    return jnp.concatenate(
+        [
+            jnp.where(head_of_lane == h, scaled, jnp.zeros_like(scaled))
+            for h in range(q.shape[1] // HEAD_DIM)
+        ],
+        0,
     )
-    row_max = total = None
+
+
+def add_keys(stacked, keys, values, row_max, total):
     for k, v in zip(keys, values):
         for start in range(0, k.shape[0], KEY_BLOCK):
             k_part, v_part = k[start : start + KEY_BLOCK], v[start : start + KEY_BLOCK]
@@ -35,11 +39,20 @@
             part = jnp.dot(rounded, summed, preferred_element_type=jnp.float32)
             total = part if row_max is None else total * jnp.exp(row_max - newer) + part
             row_max = newer
+    return row_max, total
+
+
+def finish(total, rows, width):
     out = total[:, :width] / total[:, width:]
     result = out[:rows]
-    for h in range(1, heads):
+    head_of_lane = lax.broadcasted_iota(jnp.int32, result.shape, 1) // HEAD_DIM
+    for h in range(1, width // HEAD_DIM):
         result = jnp.where(head_of_lane == h, out[h * rows : (h + 1) * rows], result)
     return result.astype(jnp.bfloat16)
+
+
+def early_chunks(chunks):
+    return 3 if chunks > 3 else 0
 
 
 def kernel(
@@ -60,11 +73,15 @@
     anchor_recv,
     relay_send,
     relay_recv,
+    max_buf,
+    sum_buf,
 ):
     frames, rows, columns = q_ref.shape
     chunks = own_sem.shape[1]
     width = columns // chunks
     anchor_slot, prior_slot = frames, frames + 1
+    early = early_chunks(chunks)
+    late = chunks - early
     z = lax.axis_index("frame")
     half = lax.axis_index("seq")
     later = (z + blocks - 1) // blocks
@@ -174,7 +191,8 @@
             prior(i, 0).start()
 
     @pl.loop(0, chunks)
-    def _(c):
+    def _(turn):
+        c = (turn + late) % chunks
         for i in range(2):
             own(i, c).start()
             for j in offsets:
@@ -203,12 +221,13 @@
                 for j in offsets:
                     relay(1, i, c, j).start()
 
-    def complete(c):
+    def complete_own(c):
         for i in range(2):
             own(i, c).wait()
             for j in offsets:
                 swap(i, c, j).wait_recv()
 
+    def complete_sent(c):
         @pl.when(z > 0)
         def _():
             for i in range(2):
@@ -216,41 +235,88 @@
                     relay(0, i, c, j).wait_recv()
                     relay(1, i, c, j).wait_recv()
 
-    block = min(rows, 512)
-    per_frame = rows // block
-    steps = frames * per_frame
-
-    def compute(c, step):
-        frame = step // per_frame
+    zero = later * anchor_slot
+
+    def whole(c, frame):
         opens = (frames - frame) // frames
         before = (frame - 1) * (1 - opens) + opens * later * prior_slot
-        zero = later * anchor_slot
-        at_rows = pl.ds(pl.multiple_of((step % per_frame) * block, block), block)
         for start in range(0, width, LANES):
             size = min(LANES, width - start)
-            if chunks > 1:
-                at = cols(c)
-            else:
-                at = pl.ds(start, size)
-            o_ref[frame, at_rows, at] = attend_columns(
-                q_ref[frame, at_rows, at],
+            at = cols(c) if chunks > 1 else pl.ds(start, size)
+            _, total = add_keys(
+                stack_heads(q_ref[frame, :, at]),
                 [k_buf[zero, :, at], k_buf[before, :, at]],
                 [v_buf[zero, :, at], v_buf[before, :, at]],
+                None,
+                None,
             )
-
-    receive(0)
+            o_ref[frame, :, at] = finish(total, rows, size)
+
+    def begin(c, frame):
+        at = cols(c)
+        row_max, total = add_keys(
+            stack_heads(q_ref[frame, :, at]),
+            [k_buf[frame - 1, :, at]],
+            [v_buf[frame - 1, :, at]],
+            None,
+            None,
+        )
+        max_buf[c - late, frame - 1] = row_max
+        sum_buf[c - late, frame - 1] = total
+
+    def close(c, frame):
+        at = cols(c)
+        _, total = add_keys(
+            stack_heads(q_ref[frame, :, at]),
+            [k_buf[zero, :, at]],
+            [v_buf[zero, :, at]],
+            max_buf[c - late, frame - 1],
+            sum_buf[c - late, frame - 1],
+        )
+        o_ref[frame, :, at] = finish(total, rows, width)
+
+    if early:
+
+        @pl.loop(0, early)
+        def _(turn):
+            complete_own(turn + late)
+
+            @pl.loop(1, frames)
+            def _(frame):
+                begin(turn + late, frame)
+
+            @pl.when((turn == z - 1) | ((turn == early - 1) & (z > early)))
+            def _():
+                receive(0)
+    else:
+        receive(0)
 
     @pl.loop(0, chunks)
     def _(c):
-        complete(c)
-
-        @pl.loop(0, steps)
-        def _(step):
-            @pl.when((step == steps // 2) & (c + 1 < chunks))
+        @pl.when(c < late)
+        def _():
+            complete_own(c)
+
+        complete_sent(c)
+
+        @pl.loop(0, frames)
+        def _(frame):
+            @pl.when((frame == frames // 2) & (c + 1 < chunks))
             def _():
                 receive(c + 1)
 
-            compute(c, step)
+            if early:
+                ready = (c >= late) & (frame > 0)
+
+                @pl.when(ready)
+                def _():
+                    close(c, frame)
+
+                @pl.when(jnp.logical_not(ready))
+                def _():
+                    whole(c, frame)
+            else:
+                whole(c, frame)
 
     @pl.loop(0, chunks)
     def _(c):
@@ -275,6 +341,8 @@
     chunks = columns // LANES if columns % LANES == 0 else 1
     held = pltpu.VMEM((frames + 2, rows * halves, columns), queries.dtype)
     dma = pltpu.SemaphoreType.DMA
+    early = early_chunks(chunks)
+    kept = (early, frames - 1, rows * LANES // HEAD_DIM) if early else (1, 1, 8)
     plain = dma((2, chunks))
     across = dma((2, chunks, halves - 1))
     relays = dma((2, 2, chunks, halves - 1))
@@ -297,6 +365,8 @@
             plain,
             relays,
             relays,
+            pltpu.VMEM(kept + (1,), jnp.float32),
+            pltpu.VMEM(kept + (2 * LANES,), jnp.float32),
         ],
         compiler_params=pltpu.CompilerParams(
             collective_id=0, has_side_effects=True, vmem_limit_bytes=56 * 1024 * 1024

time: 101 us -> 110 us (1.089)
  Pallas kernels: 97.1 us -> 107 us
    pallas_call x1, Pallas kernels: 97.1 us -> 107 us  [local(): pl.pallas_call(functools.partial(kernel, blocks, halves), out_shape=jax.S...]
where the time goes in v3:
time: 110 us
  Pallas kernels  107 us (97%)
  local copies, waits for them, and re-layouts  3.46 us (3%)
    pallas_call x1, Pallas kernels, local(): pl.pallas_call(functools.partial(kernel, blocks, halves), out_shape=jax.S...  107 us
    unnamed x1, local copies, waits for them, and re-layouts  3.46 us

profile of v3, /device:TPU:24, one launch (start us, length us, event | category | flops | bytes accessed | tf_op | source)
XLA Modules:
  0.0 110.0 jit_solution(10776186284179151793)
XLA Ops:
  0.0 106.5 %shard_map.37 = bf16[4,512,640]{2,1,0:T(8,128)(2,1)} custom-call(bf16[4,512,640]{2,1,0:T(8,128)(2,1)} %q_ref.1, bf16[4,512,640]{2,1,0:T(8,128)(2,1)} %k_ref.1, bf16[4,512,640]{2,1,0:T(8,128)(2,1)} %v_ref.1), custom_call_target="tpu_custom_call" | custom-call | tf_op jit(solution)/shard_map/pallas_call | solution.py:351
  106.5 3.5 %copy.5 = bf16[4,512,640]{2,1,0:T(8,128)(2,1)} copy(bf16[4,512,640]{2,1,0:T(8,128)(2,1)} %shard_map.37) | data formatting | bytes 5242880

commit v4 on v2

--- a/solution.py
+++ b/solution.py
@@ -159,14 +159,15 @@
         )
     pl.semaphore_wait(barrier, later + 1 - (z + 1) // blocks + halves - 1)
 
+    def send_first(c):
+        for i in range(2):
+            anchor(i, c, True).start()
+        for i in range(2):
+            prior(i, c).start()
+
     @pl.when(first & sends_on)
     def _():
-        @pl.loop(0, chunks)
-        def _(c):
-            for i in range(2):
-                anchor(i, c, True).start()
-            for i in range(2):
-                prior(i, c).start()
+        send_first(0)
 
     @pl.when((z > 0) & sends_on)
     def _():
@@ -246,9 +247,13 @@
 
         @pl.loop(0, steps)
         def _(step):
-            @pl.when((step == steps // 2) & (c + 1 < chunks))
+            @pl.when((step == steps // 2 - 1 + later) & (c + 1 < chunks))
             def _():
                 receive(c + 1)
+
+                @pl.when(first & sends_on)
+                def _():
+                    send_first(c + 1)
 
             compute(c, step)
 

time: 101 us -> 101 us (level)
  no operation moved by 1% of the time
where the time goes in v4:
time: 101 us
  Pallas kernels  97.2 us (96%)
  local copies, waits for them, and re-layouts  3.46 us (3%)
    pallas_call x1, Pallas kernels, local(): pl.pallas_call(functools.partial(kernel, blocks, halves), out_shape=jax.S...  97.2 us
    unnamed x1, local copies, waits for them, and re-layouts  3.46 us

profile of v4, /device:TPU:24, one launch (start us, length us, event | category | flops | bytes accessed | tf_op | source)
XLA Modules:
  0.0 100.7 jit_solution(3307557110657932129)
XLA Ops:
  0.0 97.2 %shard_map.37 = bf16[4,512,640]{2,1,0:T(8,128)(2,1)} custom-call(bf16[4,512,640]{2,1,0:T(8,128)(2,1)} %q_ref.1, bf16[4,512,640]{2,1,0:T(8,128)(2,1)} %k_ref.1, bf16[4,512,640]{2,1,0:T(8,128)(2,1)} %v_ref.1), custom_call_target="tpu_custom_call" | custom-call | tf_op jit(solution)/shard_map/pallas_call | solution.py:288
  97.2 3.5 %copy.5 = bf16[4,512,640]{2,1,0:T(8,128)(2,1)} copy(bf16[4,512,640]{2,1,0:T(8,128)(2,1)} %shard_map.37) | data formatting | bytes 5242880
